TPU v7x, 256 devices: a whole 4x4x8 slice. The times are simulated.
256 devices in a mesh: sec: 2 (over x_hi), col: 8 (over y, x_lo), elem: 16 (over z, core).
Axes of the slice: x: 4 (x_hi: 2, x_lo: 2; x = x_hi * 2 + x_lo), y: 4, z: 8, core: 2. Of those that a mesh axis runs over, the one named last changes fastest.
Arguments:
- probes: float32 [256, 96, 256], P('col', 'elem'), may hold values from -6 to 6
- jacobian: float32 [2, 96, 7, 256, 256], P('sec', 'elem'), may hold values from -0.0625 to 0.0625
- neighbors: int32 [96, 7], P('elem'), may hold values from 0 to 95, as said below
- stations: int32 [1024], P('elem'), may hold values from 0 to 95, as said below
- obs_weights: float32 [1024, 256], P('elem'), may hold values from -0.75 to 0.75
Outputs:
- hess_probes: float32 [256, 96, 256], P('col', 'elem', 'sec')
- gram: float32 [256, 256], P('col')
Inputs may be any that keep to these rules, and one draw needn't show every extreme that they name: `neighbors`: row e lists the 7 elements e - 3 to e + 3, taken modulo 96, each once, in an order drawn for each row. Station i lies in one of the 6 elements from (i // 64) * 6 on; every element holds one or more stations.
All inputs are finite; a program needn't handle non-finite values.
Results may differ from a plain program's by a relative error of at most 0.0001.
Values sent between devices are 32-bit elements; how exact they have to be, the bound alone decides.
No kernel may reach another device: no remote copies, remote signals or barrier semaphores. Data moves between devices by JAX's collectives and lax.ppermute only.
A program may use at most 64 MiB of HBM per device.

v0:
```python
import jax
import jax.numpy as jnp
from jax import lax
from jax.sharding import PartitionSpec as P

NBRS = 7
STEPS = 2
PRECISE = lax.Precision.HIGHEST


def with_halo(shard, sides, width):
    for axis, dim in sides:
        devices, length = (lax.axis_size(axis), shard.shape[dim])
        up = [(i, (i + 1) % devices) for i in range(devices)]
        down = [(j, i) for i, j in up]
        last = lax.slice_in_dim(shard, length - width, length, axis=dim)
        leading = lax.slice_in_dim(shard, 0, width, axis=dim)
        before = lax.ppermute(last, axis, up)
        after = lax.ppermute(leading, axis, down)
        shard = jnp.concatenate([before, shard, after], axis=dim)
    return shard


def from_behind(value, axis, steps):
    count = lax.axis_size(axis)
    pairs = [(source, (source + steps) % count) for source in range(count)]
    return lax.ppermute(value, axis, pairs)


def from_behind_2(value, axis, steps):
    count = lax.axis_size(axis)
    leading, last = (max(0, -steps), min(count, count - steps))
    return lax.ppermute(value, axis, [(source, source + steps) for source in range(leading, last)])


def tangent_pass(vector, blocks, lookup, radius):
    column_count, elem_count, dof_count = vector.shape
    for repeat in range(STEPS):
        extended = with_halo(vector, (("elem", 1),), radius)
        gathered = jnp.take(extended, lookup, axis=1).reshape(
            column_count, elem_count, NBRS, dof_count
        )
        vector = vector + jnp.einsum("cekI,ekJI->ceJ", gathered, blocks, precision=PRECISE)
    return vector


def adjoint_pass(vector, blocks, scatter_table, radius):
    column_count, elem_count, dof_count = vector.shape
    for repeat in range(STEPS):
        products = jnp.einsum("ceJ,ekJI->cekI", vector, blocks, precision=PRECISE)
        flattened = products.reshape(column_count, elem_count * NBRS, dof_count)
        extended = jnp.einsum("cxI,xy->cyI", flattened, scatter_table, precision=PRECISE)
        left_rim = extended[:, :radius]
        right_rim = extended[:, elem_count + radius :]
        from_right = from_behind(left_rim, "elem", -1)
        from_left = from_behind(right_rim, "elem", 1)
        centre = extended[:, radius : radius + elem_count]
        centre = centre.at[:, :radius].add(from_left)
        centre = centre.at[:, elem_count - radius :].add(from_right)
        vector = vector + centre
    return vector


def observe(vector, station_table, obs_weights):
    sampled = jnp.einsum("se,ceI->csI", station_table, vector, precision=PRECISE)
    readings = jnp.einsum("csI,sI->cs", sampled, obs_weights, precision=PRECISE)
    weighted = readings[:, :, None] * obs_weights[None, :, :]
    return jnp.einsum("csI,se->ceI", weighted, station_table, precision=PRECISE)


def per_device(probes, jacobian, neighbors, stations, obs_weights):
    column_count, elem_count, dof_count = probes.shape
    radius = (NBRS - 1) // 2
    elem_total = elem_count * lax.axis_size("elem")
    first_elem = lax.axis_index("elem") * elem_count
    lookup = ((neighbors - first_elem + radius) % elem_total).reshape(-1)
    ext_ids = jnp.arange(elem_count + 2 * radius, dtype=jnp.int32)
    scatter_table = (lookup[:, None] == ext_ids[None, :]).astype(jnp.float32)
    local_ids = jnp.arange(elem_count, dtype=jnp.int32)
    station_table = ((stations - first_elem)[:, None] == local_ids[None, :]).astype(jnp.float32)
    segment_index = lax.axis_index("sec")
    leading = segment_index == 0
    half_order = dof_count // 2
    blocks = jacobian[0]
    batch_count = 1
    batch_list = [probes]
    rounds = batch_count + 1
    stored = []
    incoming = jnp.zeros_like(batch_list[0])
    for round_number in range(rounds):
        start_vector = batch_list[min(round_number, batch_count - 1)]
        inputs = jnp.where(leading, start_vector, incoming)
        output = tangent_pass(inputs, blocks, lookup, radius)
        stored.append(output)
        if round_number + 1 < rounds:
            incoming = from_behind_2(output, "sec", 1)
    results = []
    returning = jnp.zeros_like(batch_list[0])
    for round_number in range(rounds):
        state_now = jnp.where(
            leading, stored[max(round_number - 1, 0)], stored[min(round_number + 1, rounds - 1)]
        )
        inputs = returning + observe(state_now, station_table, obs_weights)
        output = adjoint_pass(inputs, blocks, scatter_table, radius)
        if round_number >= 1:
            results.append(output)
        if round_number + 1 < rounds:
            returning = from_behind_2(output, "sec", -1)
    hessian_all = results[0]
    upper_half = from_behind_2(hessian_all[:, :, half_order:], "sec", 1)
    hess_local = jnp.where(leading, hessian_all[:, :, :half_order], upper_half)
    probe_half = lax.dynamic_slice_in_dim(probes, segment_index * half_order, half_order, 2)
    scaling = 1.0 / (elem_total * dof_count)
    shard_piece = lax.all_gather(hess_local, "col", axis=0, tiled=True)
    flat_piece = shard_piece.reshape(shard_piece.shape[0], -1)
    partial_gram = jnp.einsum(
        "ax,bx->ab", probe_half.reshape(column_count, -1), flat_piece, precision=PRECISE
    )
    gram = lax.psum(partial_gram, ("sec", "elem")) * scaling
    return (hess_local, gram)


def solution(mesh):
    in_specs = (
        P("col", "elem", None),
        P("sec", "elem", None, None, None),
        P("elem", None),
        P("elem"),
        P("elem", None),
    )
    out_specs = (P("col", "elem", "sec"), P("col", None))
    return jax.shard_map(
        per_device, mesh=mesh, in_specs=in_specs, out_specs=out_specs, check_vma=False
    )
```

profile of v0, /device:TPU:6, one launch (start us, length us, event | category | flops | bytes accessed | tf_op | source)
XLA Modules:
  0.0 337.1 jit_solution(581083055440860766)
XLA Ops:
  0.7 5.3 %collective-permute-start.1 = (f32[32,3,256]{2,0,1:T(8,128)S(1)}, f32[32,3,256]{2,0,1:T(8,128)S(1)}, u32[]{:S(2)}, u32[]{:S(2)}) collective-permute-start(f32[32,3,256]{2,0,1:T(8,128)S(1)} %get-tuple-element.120), channel_id=1, source_target_pairs={{1,0},{2,1},{3,2},{4,3},{5,4},{6,5},{7,6},{8,7},{9,8},{10,9},{11,1... | collective-permute-start | bytes 294920 | tf_op jit(solution)/shard_map/ppermute | solution.py:19
  9.1 12.6 %fusion.61 = f32[32,6,256]{2,0,1:T(8,128)S(1)} fusion(f32[32,6,256]{2,0,1:T(8,128)S(1)} %broadcast_select_fusion.4, f32[32,6,7,256]{3,0,2,1:T(8,128)S(1)} %bitcast.149, f32[1,6,7,256,256]{4,3,2,1,0:T(8,128)} %param.24), kind=kOutput, calls=%fused_computation.44 | convolution fusion | flops 1057013760 | bytes 12779520 | tf_op jit(solution)/shard_map/cekI,ekJI->ceJ/dot_general | solution.py:43
  21.8 3.0 collective-permute-start.3
  28.0 12.7 %fusion.58 = f32[32,6,256]{2,0,1:T(8,128)S(1)} fusion(f32[32,6,256]{2,0,1:T(8,128)S(1)} %fusion.61, f32[32,6,7,256]{3,0,2,1:T(8,128)S(1)} %bitcast.150, f32[1,6,7,256,256]{4,3,2,1,0:T(8,128)} %param.24), kind=kOutput, calls=%fused_computation.43 | convolution fusion | flops 1057013760 | bytes 12779520 | tf_op jit(solution)/shard_map/cekI,ekJI->ceJ/dot_general | solution.py:43
  42.4 7.3 %collective-permute-done.4 = f32[32,6,256]{2,0,1:T(8,128)S(1)} collective-permute-done((f32[32,6,256]{2,0,1:T(8,128)S(1)}, f32[32,6,256]{2,0,1:T(8,128)S(1)}, u32[]{:S(2)}, u32[]{:S(2)}) %collective-permute-start.4) | collective-permute-done | bytes 196640 | tf_op jit(solution)/shard_map/ppermute | solution.py:33
  49.8 2.9 collective-permute-start.6
  55.9 12.6 %fusion.55 = f32[32,6,256]{2,0,1:T(8,128)S(1)} fusion(f32[32,6,256]{2,0,1:T(8,128)S(1)} %broadcast_select_fusion.5, f32[32,6,7,256]{3,0,2,1:T(8,128)S(1)} %bitcast.151, f32[1,6,7,256,256]{4,3,2,1,0:T(8,128)} %param.24), kind=kOutput, calls=%fused_computation.42 | convolution fusion | flops 1057013760 | bytes 12779520 | tf_op jit(solution)/shard_map/cekI,ekJI->ceJ/dot_general | solution.py:43
  68.6 3.0 collective-permute-start.8
  74.7 12.8 %fusion.64 = f32[32,6,256]{2,0,1:T(8,128)S(1)} fusion(f32[32,6,256]{2,0,1:T(8,128)S(1)} %fusion.58, f32[32,6,256]{2,0,1:T(8,128)S(1)} %fusion.55, f32[32,6,7,256]{3,0,2,1:T(8,128)S(1)} %bitcast.148, f32[1,6,7,256,256]{4,3,2,1,0:T(8,128)} %param.24, pred[]{:T(512)S(6)} %eq.16), kind=kOutput, calls=%fused_computation.45 | convolution fusion | flops 1057062912 | bytes 12976129 | tf_op jit(solution)/shard_map/cekI,ekJI->ceJ/dot_general | solution.py:43
  88.6 3.1 fusion.16
  92.7 9.0 %fusion.6 = f32[6,32,7,256]{3,1,2,0:T(8,128)S(1)} fusion(f32[1,6,7,256,256]{4,3,2,1,0:T(8,128)} %param.24, f32[32,6,256,1]{2,1,0,3:T(8,128)S(1)} %bitcast.143), kind=kOutput, calls=%fused_computation.10 | convolution fusion | flops 1056964608 | bytes 12582912 | tf_op jit(solution)/shard_map/ceJ,ekJI->cekI/dot_general | solution.py:50
  103.2 3.0 collective-permute-start.10
  109.6 9.0 %fusion.4 = f32[6,32,7,256]{3,1,2,0:T(8,128)S(1)} fusion(f32[1,6,7,256,256]{4,3,2,1,0:T(8,128)} %param.24, f32[32,6,256,1]{2,1,0,3:T(8,128)S(1)} %fusion.77), kind=kOutput, calls=%fused_computation.8 | convolution fusion | flops 1056964608 | bytes 12582912 | tf_op jit(solution)/shard_map/ceJ,ekJI->cekI/dot_general | solution.py:50
  120.1 3.0 collective-permute-start.12
  123.0 2.6 collective-permute-done.11
  127.9 3.9 %collective-permute-done.13 = f32[32,6,256]{2,1,0:T(8,128)S(1)} collective-permute-done((f32[32,6,256]{2,1,0:T(8,128)S(1)}, f32[32,6,256]{2,1,0:T(8,128)S(1)}, u32[]{:S(2)}, u32[]{:S(2)}) %collective-permute-start.13) | collective-permute-done | bytes 196640 | tf_op jit(solution)/shard_map/ppermute | solution.py:33
  131.8 9.2 %fusion.2 = f32[6,32,7,256]{3,1,2,0:T(8,128)S(1)} fusion(f32[1,6,7,256,256]{4,3,2,1,0:T(8,128)} %param.24, f32[32,6,256,1]{2,1,0,3:T(8,128)S(1)} %fusion.75), kind=kOutput, calls=%fused_computation.6 | convolution fusion | flops 1056964608 | bytes 12582912 | tf_op jit(solution)/shard_map/ceJ,ekJI->cekI/dot_general | solution.py:50
  142.5 3.0 collective-permute-start.15
  145.5 2.6 collective-permute-done.14
  148.9 9.0 %fusion = f32[6,32,7,256]{3,1,2,0:T(8,128)S(1)} fusion(f32[1,6,7,256,256]{4,3,2,1,0:T(8,128)} %param.24, f32[32,6,256,1]{2,1,0,3:T(8,128)S(1)} %fusion.96), kind=kOutput, calls=%fused_computation.4 | convolution fusion | flops 1056964608 | bytes 12582912 | tf_op jit(solution)/shard_map/ceJ,ekJI->cekI/dot_general | solution.py:50
  159.4 3.0 collective-permute-start.17
  167.1 7.6 %collective-permute-done.18 = f32[32,6,128]{2,1,0:T(8,128)S(1)} collective-permute-done((f32[32,6,128]{2,1,0:T(8,128)S(1)}, f32[32,6,128]{2,1,0:T(8,128)S(1)}, u32[]{:S(2)}, u32[]{:S(2)}) %collective-permute-start.18) | collective-permute-done | bytes 98336 | tf_op jit(solution)/shard_map/ppermute | solution.py:33
  174.8 32.1 %all_gather.3 = f32[256,6,128]{2,0,1:T(8,128)S(1)} all-gather(f32[32,6,128]{2,0,1:T(8,128)S(1)} %copy.37), channel_id=1, replica_groups=mesh['sec'=2,'col'=8,'elem'=16] {'col'}, dimensions={0}, use_global_device_ids=true | all-gather | bytes 884736 | tf_op jit(solution)/shard_map/all_gather | solution.py:114
  207.7 128.5 %psum.7 = f32[32,256]{1,0:T(8,128)S(1)} all-reduce(f32[32,256]{1,0:T(8,128)S(1)} %convolution_bitcast_fusion.1), channel_id=1, replica_groups=mesh['sec'=2,'col'=8,'elem'=16] {'sec','elem'}, use_global_device_ids=true, to_apply=%region_0.2 | all-reduce | flops 8192 | bytes 65536 | tf_op jit(solution)/shard_map/psum | solution.py:119
  (98 shorter events, 34.8 us)
Async XLA Ops:
  0.7 7.6 %collective-permute-start = (f32[32,3,256]{2,0,1:T(8,128)S(1)}, f32[32,3,256]{2,0,1:T(8,128)S(1)}, u32[]{:S(2)}, u32[]{:S(2)}) collective-permute-start(f32[32,3,256]{2,0,1:T(8,128)S(1)} %get-tuple-element.119), channel_id=1, source_target_pairs={{0,1},{1,2},{2,3},{3,4},{4,5},{5,6},{6,7},{7,8},{8,9},{9,10},{10,1... | collective-permute-start | bytes 294920 | tf_op jit(solution)/shard_map/ppermute | solution.py:18
  0.7 7.6 %collective-permute-start.1 = (f32[32,3,256]{2,0,1:T(8,128)S(1)}, f32[32,3,256]{2,0,1:T(8,128)S(1)}, u32[]{:S(2)}, u32[]{:S(2)}) collective-permute-start(f32[32,3,256]{2,0,1:T(8,128)S(1)} %get-tuple-element.120), channel_id=1, source_target_pairs={{1,0},{2,1},{3,2},{4,3},{5,4},{6,5},{7,6},{8,7},{9,8},{10,9},{11,1... | collective-permute-start | bytes 294920 | tf_op jit(solution)/shard_map/ppermute | solution.py:19
  21.8 5.3 %collective-permute-start.2 = (f32[32,3,256]{2,0,1:T(8,128)S(1)}, f32[32,3,256]{2,0,1:T(8,128)S(1)}, u32[]{:S(2)}, u32[]{:S(2)}) collective-permute-start(f32[32,3,256]{2,0,1:T(8,128)S(1)} %get-tuple-element.117), channel_id=1, source_target_pairs={{0,1},{1,2},{2,3},{3,4},{4,5},{5,6},{6,7},{7,8},{8,9},{9,10},{10,1... | collective-permute-start | bytes 294920 | tf_op jit(solution)/shard_map/ppermute | solution.py:18
  21.8 5.3 %collective-permute-start.3 = (f32[32,3,256]{2,0,1:T(8,128)S(1)}, f32[32,3,256]{2,0,1:T(8,128)S(1)}, u32[]{:S(2)}, u32[]{:S(2)}) collective-permute-start(f32[32,3,256]{2,0,1:T(8,128)S(1)} %get-tuple-element.118), channel_id=1, source_target_pairs={{1,0},{2,1},{3,2},{4,3},{5,4},{6,5},{7,6},{8,7},{9,8},{10,9},{11,1... | collective-permute-start | bytes 294920 | tf_op jit(solution)/shard_map/ppermute | solution.py:19
  28.0 21.8 %copy-start = (f32[32,6,256]{2,0,1:T(8,128)S(1)}, f32[32,6,256]{2,0,1:T(8,128)}, u32[]{:S(2)}) copy-start(f32[32,6,256]{2,0,1:T(8,128)} %param.23) | copy-start | bytes 589828
  40.7 9.1 %collective-permute-start.4 = (f32[32,6,256]{2,0,1:T(8,128)S(1)}, f32[32,6,256]{2,0,1:T(8,128)S(1)}, u32[]{:S(2)}, u32[]{:S(2)}) collective-permute-start(f32[32,6,256]{2,0,1:T(8,128)S(1)} %fusion.58), channel_id=1, source_target_pairs={{0,128},{1,129},{2,130},{3,131},{4,132},{5,133},{6,134},{7,135},{8... | collective-permute-start | bytes 589832 | tf_op jit(solution)/shard_map/ppermute | solution.py:33
  49.8 5.3 %collective-permute-start.5 = (f32[32,3,256]{2,0,1:T(8,128)S(1)}, f32[32,3,256]{2,0,1:T(8,128)S(1)}, u32[]{:S(2)}, u32[]{:S(2)}) collective-permute-start(f32[32,3,256]{2,0,1:T(8,128)S(1)} %get-tuple-element.115), channel_id=1, source_target_pairs={{0,1},{1,2},{2,3},{3,4},{4,5},{5,6},{6,7},{7,8},{8,9},{9,10},{10,1... | collective-permute-start | bytes 294920 | tf_op jit(solution)/shard_map/ppermute | solution.py:18
  49.8 5.2 %collective-permute-start.6 = (f32[32,3,256]{2,0,1:T(8,128)S(1)}, f32[32,3,256]{2,0,1:T(8,128)S(1)}, u32[]{:S(2)}, u32[]{:S(2)}) collective-permute-start(f32[32,3,256]{2,0,1:T(8,128)S(1)} %get-tuple-element.116), channel_id=1, source_target_pairs={{1,0},{2,1},{3,2},{4,3},{5,4},{6,5},{7,6},{8,7},{9,8},{10,9},{11,1... | collective-permute-start | bytes 294920 | tf_op jit(solution)/shard_map/ppermute | solution.py:19
  55.9 15.7 %copy-start.3 = (s32[64]{0:T(128)S(1)}, s32[64]{0:T(128)}, u32[]{:S(2)}) copy-start(s32[64]{0:T(128)} %param.26) | copy-start | bytes 772
  68.6 5.3 %collective-permute-start.7 = (f32[32,3,256]{2,0,1:T(8,128)S(1)}, f32[32,3,256]{2,0,1:T(8,128)S(1)}, u32[]{:S(2)}, u32[]{:S(2)}) collective-permute-start(f32[32,3,256]{2,0,1:T(8,128)S(1)} %get-tuple-element.113), channel_id=1, source_target_pairs={{0,1},{1,2},{2,3},{3,4},{4,5},{5,6},{6,7},{7,8},{8,9},{9,10},{10,1... | collective-permute-start | bytes 294920 | tf_op jit(solution)/shard_map/ppermute | solution.py:18
  68.6 5.2 %collective-permute-start.8 = (f32[32,3,256]{2,0,1:T(8,128)S(1)}, f32[32,3,256]{2,0,1:T(8,128)S(1)}, u32[]{:S(2)}, u32[]{:S(2)}) collective-permute-start(f32[32,3,256]{2,0,1:T(8,128)S(1)} %get-tuple-element.114), channel_id=1, source_target_pairs={{1,0},{2,1},{3,2},{4,3},{5,4},{6,5},{7,6},{8,7},{9,8},{10,9},{11,1... | collective-permute-start | bytes 294920 | tf_op jit(solution)/shard_map/ppermute | solution.py:19
  87.5 1.0 copy-start.2
  103.1 5.6 %collective-permute-start.9 = (f32[32,3,256]{2,1,0:T(4,128)S(1)}, f32[32,3,256]{2,1,0:T(4,128)S(1)}, u32[]{:S(2)}, u32[]{:S(2)}) collective-permute-start(f32[32,3,256]{2,1,0:T(4,128)S(1)} %get-tuple-element.112), channel_id=1, source_target_pairs={{0,1},{1,2},{2,3},{3,4},{4,5},{5,6},{6,7},{7,8},{8,9},{9,10},{10,1... | collective-permute-start | bytes 294920 | tf_op jit(solution)/shard_map/ppermute | solution.py:27
  103.2 5.9 %collective-permute-start.10 = (f32[32,3,256]{2,1,0:T(4,128)S(1)}, f32[32,3,256]{2,1,0:T(4,128)S(1)}, u32[]{:S(2)}, u32[]{:S(2)}) collective-permute-start(f32[32,3,256]{2,1,0:T(4,128)S(1)} %get-tuple-element.111), channel_id=1, source_target_pairs={{0,15},{1,0},{2,1},{3,2},{4,3},{5,4},{6,5},{7,6},{8,7},{9,8},{10,9... | collective-permute-start | bytes 294920 | tf_op jit(solution)/shard_map/ppermute | solution.py:27
  120.0 5.6 %collective-permute-start.11 = (f32[32,3,256]{2,1,0:T(4,128)S(1)}, f32[32,3,256]{2,1,0:T(4,128)S(1)}, u32[]{:S(2)}, u32[]{:S(2)}) collective-permute-start(f32[32,3,256]{2,1,0:T(4,128)S(1)} %get-tuple-element.110), channel_id=1, source_target_pairs={{0,1},{1,2},{2,3},{3,4},{4,5},{5,6},{6,7},{7,8},{8,9},{9,10},{10,1... | collective-permute-start | bytes 294920 | tf_op jit(solution)/shard_map/ppermute | solution.py:27
  120.1 5.9 %collective-permute-start.12 = (f32[32,3,256]{2,1,0:T(4,128)S(1)}, f32[32,3,256]{2,1,0:T(4,128)S(1)}, u32[]{:S(2)}, u32[]{:S(2)}) collective-permute-start(f32[32,3,256]{2,1,0:T(4,128)S(1)} %get-tuple-element.109), channel_id=1, source_target_pairs={{0,15},{1,0},{2,1},{3,2},{4,3},{5,4},{6,5},{7,6},{8,7},{9,8},{10,9... | collective-permute-start | bytes 294920 | tf_op jit(solution)/shard_map/ppermute | solution.py:27
  126.4 5.3 %collective-permute-start.13 = (f32[32,6,256]{2,1,0:T(8,128)S(1)}, f32[32,6,256]{2,1,0:T(8,128)S(1)}, u32[]{:S(2)}, u32[]{:S(2)}) collective-permute-start(f32[32,6,256]{2,1,0:T(8,128)S(1)} %fusion.76), channel_id=1, source_target_pairs={{128,0},{129,1},{130,2},{131,3},{132,4},{133,5},{134,6},{135,7},{1... | collective-permute-start | bytes 589832 | tf_op jit(solution)/shard_map/ppermute | solution.py:33
  142.5 5.6 %collective-permute-start.14 = (f32[32,3,256]{2,1,0:T(4,128)S(1)}, f32[32,3,256]{2,1,0:T(4,128)S(1)}, u32[]{:S(2)}, u32[]{:S(2)}) collective-permute-start(f32[32,3,256]{2,1,0:T(4,128)S(1)} %get-tuple-element.108), channel_id=1, source_target_pairs={{0,1},{1,2},{2,3},{3,4},{4,5},{5,6},{6,7},{7,8},{8,9},{9,10},{10,1... | collective-permute-start | bytes 294920 | tf_op jit(solution)/shard_map/ppermute | solution.py:27
  142.5 5.9 %collective-permute-start.15 = (f32[32,3,256]{2,1,0:T(4,128)S(1)}, f32[32,3,256]{2,1,0:T(4,128)S(1)}, u32[]{:S(2)}, u32[]{:S(2)}) collective-permute-start(f32[32,3,256]{2,1,0:T(4,128)S(1)} %get-tuple-element.107), channel_id=1, source_target_pairs={{0,15},{1,0},{2,1},{3,2},{4,3},{5,4},{6,5},{7,6},{8,7},{9,8},{10,9... | collective-permute-start | bytes 294920 | tf_op jit(solution)/shard_map/ppermute | solution.py:27
  159.3 5.6 %collective-permute-start.16 = (f32[32,3,256]{2,1,0:T(4,128)S(1)}, f32[32,3,256]{2,1,0:T(4,128)S(1)}, u32[]{:S(2)}, u32[]{:S(2)}) collective-permute-start(f32[32,3,256]{2,1,0:T(4,128)S(1)} %get-tuple-element.106), channel_id=1, source_target_pairs={{0,1},{1,2},{2,3},{3,4},{4,5},{5,6},{6,7},{7,8},{8,9},{9,10},{10,1... | collective-permute-start | bytes 294920 | tf_op jit(solution)/shard_map/ppermute | solution.py:27
  159.4 5.9 %collective-permute-start.17 = (f32[32,3,256]{2,1,0:T(4,128)S(1)}, f32[32,3,256]{2,1,0:T(4,128)S(1)}, u32[]{:S(2)}, u32[]{:S(2)}) collective-permute-start(f32[32,3,256]{2,1,0:T(4,128)S(1)} %get-tuple-element.105), channel_id=1, source_target_pairs={{0,15},{1,0},{2,1},{3,2},{4,3},{5,4},{6,5},{7,6},{8,7},{9,8},{10,9... | collective-permute-start | bytes 294920 | tf_op jit(solution)/shard_map/ppermute | solution.py:27
  165.8 8.9 %collective-permute-start.18 = (f32[32,6,128]{2,1,0:T(8,128)S(1)}, f32[32,6,128]{2,1,0:T(8,128)S(1)}, u32[]{:S(2)}, u32[]{:S(2)}) collective-permute-start(f32[32,6,128]{2,1,0:T(8,128)S(1)} %slice.329), channel_id=1, source_target_pairs={{0,128},{1,129},{2,130},{3,131},{4,132},{5,133},{6,134},{7,135},{8... | collective-permute-start | bytes 294920 | tf_op jit(solution)/shard_map/ppermute | solution.py:33
  174.8 162.1 %copy-start.1 = (f32[32,6,128]{2,0,1:T(8,128)}, f32[32,6,128]{2,0,1:T(8,128)S(1)}, u32[]{:S(2)}) copy-start(f32[32,6,128]{2,0,1:T(8,128)S(1)} %copy.37) | copy-start | bytes 294916
where the time goes:
time: 344 us; the launch traced here: 337 us
  blocking collectives  161 us (47%)
  matrix products  98.3 us (29%)
  waiting for transfers between devices  37.5 us (11%)
  starting transfers between devices  30.7 us (9%)
  local copies, waits for them, and re-layouts  5.62 us (2%)
    psum x1, blocking collectives, per_device(): gram = lax.psum(partial_gram, ('sec', 'elem')) * scaling  129 us
    dot_general x4, matrix products, tangent_pass(): jnp.einsum('cekI,ekJI->ceJ', gathered, blocks, precision=PRECISE)  50.8 us
    dot_general x4, matrix products, adjoint_pass(): products = jnp.einsum('ceJ,ekJI->cekI', vector, blocks, precision=PRECISE)  36.2 us
    all_gather x1, blocking collectives, per_device(): shard_piece = lax.all_gather(hess_local, 'col', axis=0, tiled=True)  32.1 us
    ppermute x3, waiting for transfers between devices, from_behind_2(): lax.ppermute(value, axis, [(source, source + steps) for source in range(l...  18.8 us
    ppermute x4, starting transfers between devices, with_halo(): after = lax.ppermute(leading, axis, down)  14.2 us
    ppermute x8, starting transfers between devices, from_behind(): return lax.ppermute(value, axis, pairs)  11.9 us
    ppermute x8, waiting for transfers between devices, from_behind(): return lax.ppermute(value, axis, pairs)  10.4 us
  transfers between devices with their start and end apart: 19, of which 11 were waited for; matrix products, arithmetic and copies ran while one was open for 1% of the time, Pallas kernels for 0%

commit v1 on v0

--- a/solution.py
+++ b/solution.py
@@ -111,7 +111,9 @@
     hess_local = jnp.where(leading, hessian_all[:, :, :half_order], upper_half)
     probe_half = lax.dynamic_slice_in_dim(probes, segment_index * half_order, half_order, 2)
     scaling = 1.0 / (elem_total * dof_count)
-    shard_piece = lax.all_gather(hess_local, "col", axis=0, tiled=True)
+    shard_piece = jnp.concatenate(
+        lax.all_to_all(jnp.stack([hess_local] * lax.axis_size("col")), "col", 0, 0), axis=0
+    )
     flat_piece = shard_piece.reshape(shard_piece.shape[0], -1)
     partial_gram = jnp.einsum(
         "ax,bx->ab", probe_half.reshape(column_count, -1), flat_piece, precision=PRECISE

time: 344 us -> 332 us (0.965)
  the two profiles are of different devices: /device:TPU:6 before, /device:TPU:2 now
where the time goes in v1:
time: 332 us; the launch traced here: 325 us
  blocking collectives  135 us (41%)
  matrix products  98.3 us (30%)
  waiting for transfers between devices  41.3 us (12%)
  starting transfers between devices  38.4 us (12%)
  local copies, waits for them, and re-layouts  7.08 us (2%)
  other arithmetic  3.71 us (1%)
    psum x1, blocking collectives, per_device(): gram = lax.psum(partial_gram, ('sec', 'elem')) * scaling  135 us
    dot_general x4, matrix products, tangent_pass(): jnp.einsum('cekI,ekJI->ceJ', gathered, blocks, precision=PRECISE)  50.8 us
    dot_general x4, matrix products, adjoint_pass(): products = jnp.einsum('ceJ,ekJI->cekI', vector, blocks, precision=PRECISE)  36.2 us
    ppermute x4, starting transfers between devices, with_halo(): after = lax.ppermute(leading, axis, down)  14.2 us
    ppermute x3, waiting for transfers between devices, from_behind_2(): lax.ppermute(value, axis, [(source, source + steps) for source in range(l...  13.7 us
    ppermute x8, starting transfers between devices, from_behind(): return lax.ppermute(value, axis, pairs)  11.9 us
    ppermute x8, waiting for transfers between devices, from_behind(): return lax.ppermute(value, axis, pairs)  10.4 us
    all_to_all x1, waiting for transfers between devices, per_device(): lax.all_to_all(jnp.stack([hess_local] * lax.axis_size('col')), 'col', 0, 0)  8.93 us
  transfers between devices with their start and end apart: 20, of which 12 were waited for; matrix products, arithmetic and copies ran while one was open for 1% of the time, Pallas kernels for 0%

profile of v1, /device:TPU:2, one launch (start us, length us, event | category | flops | bytes accessed | tf_op | source)
XLA Modules:
  0.0 325.4 jit_solution(3133910365934352897)
XLA Ops:
  1.6 5.3 %collective-permute-start.1 = (f32[32,3,256]{2,0,1:T(8,128)S(1)}, f32[32,3,256]{2,0,1:T(8,128)S(1)}, u32[]{:S(2)}, u32[]{:S(2)}) collective-permute-start(f32[32,3,256]{2,0,1:T(8,128)S(1)} %get-tuple-element.120), channel_id=1, source_target_pairs={{1,0},{2,1},{3,2},{4,3},{5,4},{6,5},{7,6},{8,7},{9,8},{10,9},{11,1... | collective-permute-start | bytes 294920 | tf_op jit(solution)/shard_map/ppermute | solution.py:19
  10.1 12.6 %fusion.61 = f32[32,6,256]{2,0,1:T(8,128)S(1)} fusion(f32[32,6,256]{2,0,1:T(8,128)S(1)} %broadcast_select_fusion.4, f32[32,6,7,256]{3,0,2,1:T(8,128)S(1)} %bitcast.158, f32[1,6,7,256,256]{4,3,2,1,0:T(8,128)} %param.24), kind=kOutput, calls=%fused_computation.44 | convolution fusion | flops 1057013760 | bytes 12779520 | tf_op jit(solution)/shard_map/cekI,ekJI->ceJ/dot_general | solution.py:43
  22.8 3.0 collective-permute-start.3
  28.9 12.7 %fusion.58 = f32[32,6,256]{2,0,1:T(8,128)S(1)} fusion(f32[32,6,256]{2,0,1:T(8,128)S(1)} %fusion.61, f32[32,6,7,256]{3,0,2,1:T(8,128)S(1)} %bitcast.159, f32[1,6,7,256,256]{4,3,2,1,0:T(8,128)} %param.24), kind=kOutput, calls=%fused_computation.43 | convolution fusion | flops 1057013760 | bytes 12779520 | tf_op jit(solution)/shard_map/cekI,ekJI->ceJ/dot_general | solution.py:43
  41.6 3.6 %collective-permute-start.4 = (f32[32,6,256]{2,0,1:T(8,128)S(1)}, f32[32,6,256]{2,0,1:T(8,128)S(1)}, u32[]{:S(2)}, u32[]{:S(2)}) collective-permute-start(f32[32,6,256]{2,0,1:T(8,128)S(1)} %fusion.58), channel_id=1, source_target_pairs={{0,128},{1,129},{2,130},{3,131},{4,132},{5,133},{6,134},{7,135},{8... | collective-permute-start | bytes 589832 | tf_op jit(solution)/shard_map/ppermute | solution.py:33
  45.2 2.7 collective-permute-done.4
  47.9 2.9 collective-permute-start.6
  54.0 12.6 %fusion.55 = f32[32,6,256]{2,0,1:T(8,128)S(1)} fusion(f32[32,6,256]{2,0,1:T(8,128)S(1)} %broadcast_select_fusion.5, f32[32,6,7,256]{3,0,2,1:T(8,128)S(1)} %bitcast.160, f32[1,6,7,256,256]{4,3,2,1,0:T(8,128)} %param.24), kind=kOutput, calls=%fused_computation.42 | convolution fusion | flops 1057013760 | bytes 12779520 | tf_op jit(solution)/shard_map/cekI,ekJI->ceJ/dot_general | solution.py:43
  66.7 3.0 collective-permute-start.8
  72.8 12.8 %fusion.64 = f32[32,6,256]{2,0,1:T(8,128)S(1)} fusion(f32[32,6,256]{2,0,1:T(8,128)S(1)} %fusion.58, f32[32,6,256]{2,0,1:T(8,128)S(1)} %fusion.55, f32[32,6,7,256]{3,0,2,1:T(8,128)S(1)} %bitcast.157, f32[1,6,7,256,256]{4,3,2,1,0:T(8,128)} %param.24, pred[]{:T(512)S(6)} %eq.16), kind=kOutput, calls=%fused_computation.45 | convolution fusion | flops 1057062912 | bytes 12976129 | tf_op jit(solution)/shard_map/cekI,ekJI->ceJ/dot_general | solution.py:43
  86.7 3.1 fusion.16
  90.8 9.0 %fusion.6 = f32[6,32,7,256]{3,1,2,0:T(8,128)S(1)} fusion(f32[1,6,7,256,256]{4,3,2,1,0:T(8,128)} %param.24, f32[32,6,256,1]{2,1,0,3:T(8,128)S(1)} %bitcast.152), kind=kOutput, calls=%fused_computation.10 | convolution fusion | flops 1056964608 | bytes 12582912 | tf_op jit(solution)/shard_map/ceJ,ekJI->cekI/dot_general | solution.py:50
  101.3 3.0 collective-permute-start.10
  107.7 9.0 %fusion.4 = f32[6,32,7,256]{3,1,2,0:T(8,128)S(1)} fusion(f32[1,6,7,256,256]{4,3,2,1,0:T(8,128)} %param.24, f32[32,6,256,1]{2,1,0,3:T(8,128)S(1)} %fusion.80), kind=kOutput, calls=%fused_computation.8 | convolution fusion | flops 1056964608 | bytes 12582912 | tf_op jit(solution)/shard_map/ceJ,ekJI->cekI/dot_general | solution.py:50
  118.2 3.0 collective-permute-start.12
  121.2 2.6 collective-permute-done.11
  125.9 8.5 %collective-permute-done.13 = f32[32,6,256]{2,1,0:T(8,128)S(1)} collective-permute-done((f32[32,6,256]{2,1,0:T(8,128)S(1)}, f32[32,6,256]{2,1,0:T(8,128)S(1)}, u32[]{:S(2)}, u32[]{:S(2)}) %collective-permute-start.13) | collective-permute-done | bytes 196640 | tf_op jit(solution)/shard_map/ppermute | solution.py:33
  134.4 9.2 %fusion.2 = f32[6,32,7,256]{3,1,2,0:T(8,128)S(1)} fusion(f32[1,6,7,256,256]{4,3,2,1,0:T(8,128)} %param.24, f32[32,6,256,1]{2,1,0,3:T(8,128)S(1)} %fusion.78), kind=kOutput, calls=%fused_computation.6 | convolution fusion | flops 1056964608 | bytes 12582912 | tf_op jit(solution)/shard_map/ceJ,ekJI->cekI/dot_general | solution.py:50
  145.1 3.0 collective-permute-start.15
  151.5 9.0 %fusion = f32[6,32,7,256]{3,1,2,0:T(8,128)S(1)} fusion(f32[1,6,7,256,256]{4,3,2,1,0:T(8,128)} %param.24, f32[32,6,256,1]{2,1,0,3:T(8,128)S(1)} %fusion.99), kind=kOutput, calls=%fused_computation.4 | convolution fusion | flops 1056964608 | bytes 12582912 | tf_op jit(solution)/shard_map/ceJ,ekJI->cekI/dot_general | solution.py:50
  162.0 3.0 collective-permute-start.17
  173.4 5.9 %all-to-all-start = ((f32[8,32,6,128]{3,1,2,0:T(8,128)}), f32[8,32,6,128]{3,1,2,0:T(8,128)S(1)}, u32[]{:S(2)}, u32[]{:S(2)}) async-start(f32[8,32,6,128]{3,1,2,0:T(8,128)} %stack.2), calls=%async_computation | async-start | bytes 1572864 | tf_op jit(solution)/shard_map/all_to_all | solution.py:115
  179.3 8.9 %all-to-all-done = f32[8,32,6,128]{3,1,2,0:T(8,128)S(1)} async-done(((f32[8,32,6,128]{3,1,2,0:T(8,128)}), f32[8,32,6,128]{3,1,2,0:T(8,128)S(1)}, u32[]{:S(2)}, u32[]{:S(2)}) %all-to-all-start) | async-done | bytes 786464 | tf_op jit(solution)/shard_map/all_to_all | solution.py:115
  189.5 135.1 %psum.7 = f32[32,256]{1,0:T(8,128)S(1)} all-reduce(f32[32,256]{1,0:T(8,128)S(1)} %fusion.69), channel_id=1, replica_groups=mesh['sec'=2,'col'=8,'elem'=16] {'sec','elem'}, use_global_device_ids=true, to_apply=%region_0.2 | all-reduce | flops 8192 | bytes 65536 | tf_op jit(solution)/shard_map/psum | solution.py:121
  (101 shorter events, 40.5 us)
Async XLA Ops:
  1.6 7.6 %collective-permute-start = (f32[32,3,256]{2,0,1:T(8,128)S(1)}, f32[32,3,256]{2,0,1:T(8,128)S(1)}, u32[]{:S(2)}, u32[]{:S(2)}) collective-permute-start(f32[32,3,256]{2,0,1:T(8,128)S(1)} %get-tuple-element.119), channel_id=1, source_target_pairs={{0,1},{1,2},{2,3},{3,4},{4,5},{5,6},{6,7},{7,8},{8,9},{9,10},{10,1... | collective-permute-start | bytes 294920 | tf_op jit(solution)/shard_map/ppermute | solution.py:18
  1.6 7.6 %collective-permute-start.1 = (f32[32,3,256]{2,0,1:T(8,128)S(1)}, f32[32,3,256]{2,0,1:T(8,128)S(1)}, u32[]{:S(2)}, u32[]{:S(2)}) collective-permute-start(f32[32,3,256]{2,0,1:T(8,128)S(1)} %get-tuple-element.120), channel_id=1, source_target_pairs={{1,0},{2,1},{3,2},{4,3},{5,4},{6,5},{7,6},{8,7},{9,8},{10,9},{11,1... | collective-permute-start | bytes 294920 | tf_op jit(solution)/shard_map/ppermute | solution.py:19
  22.7 5.3 %collective-permute-start.2 = (f32[32,3,256]{2,0,1:T(8,128)S(1)}, f32[32,3,256]{2,0,1:T(8,128)S(1)}, u32[]{:S(2)}, u32[]{:S(2)}) collective-permute-start(f32[32,3,256]{2,0,1:T(8,128)S(1)} %get-tuple-element.117), channel_id=1, source_target_pairs={{0,1},{1,2},{2,3},{3,4},{4,5},{5,6},{6,7},{7,8},{8,9},{9,10},{10,1... | collective-permute-start | bytes 294920 | tf_op jit(solution)/shard_map/ppermute | solution.py:18
  22.8 5.3 %collective-permute-start.3 = (f32[32,3,256]{2,0,1:T(8,128)S(1)}, f32[32,3,256]{2,0,1:T(8,128)S(1)}, u32[]{:S(2)}, u32[]{:S(2)}) collective-permute-start(f32[32,3,256]{2,0,1:T(8,128)S(1)} %get-tuple-element.118), channel_id=1, source_target_pairs={{1,0},{2,1},{3,2},{4,3},{5,4},{6,5},{7,6},{8,7},{9,8},{10,9},{11,1... | collective-permute-start | bytes 294920 | tf_op jit(solution)/shard_map/ppermute | solution.py:19
  28.9 19.0 %copy-start = (f32[32,6,256]{2,0,1:T(8,128)S(1)}, f32[32,6,256]{2,0,1:T(8,128)}, u32[]{:S(2)}) copy-start(f32[32,6,256]{2,0,1:T(8,128)} %param.23) | copy-start | bytes 589828
  41.6 6.3 %collective-permute-start.4 = (f32[32,6,256]{2,0,1:T(8,128)S(1)}, f32[32,6,256]{2,0,1:T(8,128)S(1)}, u32[]{:S(2)}, u32[]{:S(2)}) collective-permute-start(f32[32,6,256]{2,0,1:T(8,128)S(1)} %fusion.58), channel_id=1, source_target_pairs={{0,128},{1,129},{2,130},{3,131},{4,132},{5,133},{6,134},{7,135},{8... | collective-permute-start | bytes 589832 | tf_op jit(solution)/shard_map/ppermute | solution.py:33
  47.9 5.3 %collective-permute-start.5 = (f32[32,3,256]{2,0,1:T(8,128)S(1)}, f32[32,3,256]{2,0,1:T(8,128)S(1)}, u32[]{:S(2)}, u32[]{:S(2)}) collective-permute-start(f32[32,3,256]{2,0,1:T(8,128)S(1)} %get-tuple-element.115), channel_id=1, source_target_pairs={{0,1},{1,2},{2,3},{3,4},{4,5},{5,6},{6,7},{7,8},{8,9},{9,10},{10,1... | collective-permute-start | bytes 294920 | tf_op jit(solution)/shard_map/ppermute | solution.py:18
  47.9 5.2 %collective-permute-start.6 = (f32[32,3,256]{2,0,1:T(8,128)S(1)}, f32[32,3,256]{2,0,1:T(8,128)S(1)}, u32[]{:S(2)}, u32[]{:S(2)}) collective-permute-start(f32[32,3,256]{2,0,1:T(8,128)S(1)} %get-tuple-element.116), channel_id=1, source_target_pairs={{1,0},{2,1},{3,2},{4,3},{5,4},{6,5},{7,6},{8,7},{9,8},{10,9},{11,1... | collective-permute-start | bytes 294920 | tf_op jit(solution)/shard_map/ppermute | solution.py:19
  54.0 15.7 %copy-start.3 = (s32[64]{0:T(128)S(1)}, s32[64]{0:T(128)}, u32[]{:S(2)}) copy-start(s32[64]{0:T(128)} %param.26) | copy-start | bytes 772
  66.7 5.3 %collective-permute-start.7 = (f32[32,3,256]{2,0,1:T(8,128)S(1)}, f32[32,3,256]{2,0,1:T(8,128)S(1)}, u32[]{:S(2)}, u32[]{:S(2)}) collective-permute-start(f32[32,3,256]{2,0,1:T(8,128)S(1)} %get-tuple-element.113), channel_id=1, source_target_pairs={{0,1},{1,2},{2,3},{3,4},{4,5},{5,6},{6,7},{7,8},{8,9},{9,10},{10,1... | collective-permute-start | bytes 294920 | tf_op jit(solution)/shard_map/ppermute | solution.py:18
  66.7 5.2 %collective-permute-start.8 = (f32[32,3,256]{2,0,1:T(8,128)S(1)}, f32[32,3,256]{2,0,1:T(8,128)S(1)}, u32[]{:S(2)}, u32[]{:S(2)}) collective-permute-start(f32[32,3,256]{2,0,1:T(8,128)S(1)} %get-tuple-element.114), channel_id=1, source_target_pairs={{1,0},{2,1},{3,2},{4,3},{5,4},{6,5},{7,6},{8,7},{9,8},{10,9},{11,1... | collective-permute-start | bytes 294920 | tf_op jit(solution)/shard_map/ppermute | solution.py:19
  85.7 1.1 copy-start.2
  101.3 5.6 %collective-permute-start.9 = (f32[32,3,256]{2,1,0:T(4,128)S(1)}, f32[32,3,256]{2,1,0:T(4,128)S(1)}, u32[]{:S(2)}, u32[]{:S(2)}) collective-permute-start(f32[32,3,256]{2,1,0:T(4,128)S(1)} %get-tuple-element.112), channel_id=1, source_target_pairs={{0,1},{1,2},{2,3},{3,4},{4,5},{5,6},{6,7},{7,8},{8,9},{9,10},{10,1... | collective-permute-start | bytes 294920 | tf_op jit(solution)/shard_map/ppermute | solution.py:27
  101.3 5.9 %collective-permute-start.10 = (f32[32,3,256]{2,1,0:T(4,128)S(1)}, f32[32,3,256]{2,1,0:T(4,128)S(1)}, u32[]{:S(2)}, u32[]{:S(2)}) collective-permute-start(f32[32,3,256]{2,1,0:T(4,128)S(1)} %get-tuple-element.111), channel_id=1, source_target_pairs={{0,15},{1,0},{2,1},{3,2},{4,3},{5,4},{6,5},{7,6},{8,7},{9,8},{10,9... | collective-permute-start | bytes 294920 | tf_op jit(solution)/shard_map/ppermute | solution.py:27
  118.1 5.6 %collective-permute-start.11 = (f32[32,3,256]{2,1,0:T(4,128)S(1)}, f32[32,3,256]{2,1,0:T(4,128)S(1)}, u32[]{:S(2)}, u32[]{:S(2)}) collective-permute-start(f32[32,3,256]{2,1,0:T(4,128)S(1)} %get-tuple-element.110), channel_id=1, source_target_pairs={{0,1},{1,2},{2,3},{3,4},{4,5},{5,6},{6,7},{7,8},{8,9},{9,10},{10,1... | collective-permute-start | bytes 294920 | tf_op jit(solution)/shard_map/ppermute | solution.py:27
  118.2 5.9 %collective-permute-start.12 = (f32[32,3,256]{2,1,0:T(4,128)S(1)}, f32[32,3,256]{2,1,0:T(4,128)S(1)}, u32[]{:S(2)}, u32[]{:S(2)}) collective-permute-start(f32[32,3,256]{2,1,0:T(4,128)S(1)} %get-tuple-element.109), channel_id=1, source_target_pairs={{0,15},{1,0},{2,1},{3,2},{4,3},{5,4},{6,5},{7,6},{8,7},{9,8},{10,9... | collective-permute-start | bytes 294920 | tf_op jit(solution)/shard_map/ppermute | solution.py:27
  124.6 9.8 %collective-permute-start.13 = (f32[32,6,256]{2,1,0:T(8,128)S(1)}, f32[32,6,256]{2,1,0:T(8,128)S(1)}, u32[]{:S(2)}, u32[]{:S(2)}) collective-permute-start(f32[32,6,256]{2,1,0:T(8,128)S(1)} %fusion.79), channel_id=1, source_target_pairs={{128,0},{129,1},{130,2},{131,3},{132,4},{133,5},{134,6},{135,7},{1... | collective-permute-start | bytes 589832 | tf_op jit(solution)/shard_map/ppermute | solution.py:33
  145.0 5.6 %collective-permute-start.14 = (f32[32,3,256]{2,1,0:T(4,128)S(1)}, f32[32,3,256]{2,1,0:T(4,128)S(1)}, u32[]{:S(2)}, u32[]{:S(2)}) collective-permute-start(f32[32,3,256]{2,1,0:T(4,128)S(1)} %get-tuple-element.108), channel_id=1, source_target_pairs={{0,1},{1,2},{2,3},{3,4},{4,5},{5,6},{6,7},{7,8},{8,9},{9,10},{10,1... | collective-permute-start | bytes 294920 | tf_op jit(solution)/shard_map/ppermute | solution.py:27
  145.1 5.9 %collective-permute-start.15 = (f32[32,3,256]{2,1,0:T(4,128)S(1)}, f32[32,3,256]{2,1,0:T(4,128)S(1)}, u32[]{:S(2)}, u32[]{:S(2)}) collective-permute-start(f32[32,3,256]{2,1,0:T(4,128)S(1)} %get-tuple-element.107), channel_id=1, source_target_pairs={{0,15},{1,0},{2,1},{3,2},{4,3},{5,4},{6,5},{7,6},{8,7},{9,8},{10,9... | collective-permute-start | bytes 294920 | tf_op jit(solution)/shard_map/ppermute | solution.py:27
  161.9 5.6 %collective-permute-start.16 = (f32[32,3,256]{2,1,0:T(4,128)S(1)}, f32[32,3,256]{2,1,0:T(4,128)S(1)}, u32[]{:S(2)}, u32[]{:S(2)}) collective-permute-start(f32[32,3,256]{2,1,0:T(4,128)S(1)} %get-tuple-element.106), channel_id=1, source_target_pairs={{0,1},{1,2},{2,3},{3,4},{4,5},{5,6},{6,7},{7,8},{8,9},{9,10},{10,1... | collective-permute-start | bytes 294920 | tf_op jit(solution)/shard_map/ppermute | solution.py:27
  162.0 5.9 %collective-permute-start.17 = (f32[32,3,256]{2,1,0:T(4,128)S(1)}, f32[32,3,256]{2,1,0:T(4,128)S(1)}, u32[]{:S(2)}, u32[]{:S(2)}) collective-permute-start(f32[32,3,256]{2,1,0:T(4,128)S(1)} %get-tuple-element.105), channel_id=1, source_target_pairs={{0,15},{1,0},{2,1},{3,2},{4,3},{5,4},{6,5},{7,6},{8,7},{9,8},{10,9... | collective-permute-start | bytes 294920 | tf_op jit(solution)/shard_map/ppermute | solution.py:27
  168.4 4.0 %collective-permute-start.18 = (f32[32,6,128]{2,1,0:T(8,128)S(1)}, f32[32,6,128]{2,1,0:T(8,128)S(1)}, u32[]{:S(2)}, u32[]{:S(2)}) collective-permute-start(f32[32,6,128]{2,1,0:T(8,128)S(1)} %slice.329), channel_id=1, source_target_pairs={{0,128},{1,129},{2,130},{3,131},{4,132},{5,133},{6,134},{7,135},{8... | collective-permute-start | bytes 294920 | tf_op jit(solution)/shard_map/ppermute | solution.py:33
  172.4 16.3 %copy-start.1 = (f32[32,6,128]{2,0,1:T(8,128)}, f32[32,6,128]{2,0,1:T(8,128)S(1)}, u32[]{:S(2)}) copy-start(f32[32,6,128]{2,0,1:T(8,128)S(1)} %copy.38) | copy-start | bytes 294916
  173.4 14.9 %all-to-all-start = ((f32[8,32,6,128]{3,1,2,0:T(8,128)}), f32[8,32,6,128]{3,1,2,0:T(8,128)S(1)}, u32[]{:S(2)}, u32[]{:S(2)}) async-start(f32[8,32,6,128]{3,1,2,0:T(8,128)} %stack.2), calls=%async_computation | async-start | bytes 1572864 | tf_op jit(solution)/shard_map/all_to_all | solution.py:115
